TPU v7x, 32 devices: a whole 2x2x4 slice. The times are simulated.
32 devices in a mesh: ctx: 4 (over y, core), exp: 8 (over z, x).
Axes of the slice: x: 2, y: 2, z: 4, core: 2. Of those that a mesh axis runs over, the one named last changes fastest.
Arguments:
- layer_input: bfloat16 [8, 1536, 2048], P('exp', 'ctx'), may hold values from -30 to 30
- block_ids: int32 [8, 8], P('exp'), may hold values from 0 to 7, as said below
- routes: int32 [8, 1536, 8], P('exp', 'ctx'), may hold values from 0 to 15, all different within a row
- w_query: bfloat16 [2048, 2048], P('exp'), may hold values from -0.125 to 0.125
- w_key: bfloat16 [2048, 2048], P('exp'), may hold values from -0.125 to 0.125
- w_value: bfloat16 [2048, 2048], P('exp'), may hold values from -0.125 to 0.125
- w_output: bfloat16 [2048, 2048], P('exp'), may hold values from -2 to 2
- w_router: bfloat16 [2048, 16], P('exp'), may hold values from -0.0625 to 0.0625
- norm_gains: bfloat16 [2048, 4], P('exp'), may hold values from 0.25 to 1.75
- w_gate_up: bfloat16 [16, 4096, 1024], P('exp', None, 'ctx'), may hold values from -0.125 to 0.125
- w_down: bfloat16 [16, 2048, 1024], P('exp', None, 'ctx'), may hold values from -4 to 4
- d_out: bfloat16 [8, 1536, 2048], P('exp', 'ctx'), may hold values from -6 to 6
Outputs:
- output: bfloat16 [8, 1536, 2048], P('exp', 'ctx')
- d_x: float32 [8, 1536, 2048], P('exp', 'ctx')
- g_query: float32 [2048, 2048], P('exp')
- g_key: float32 [2048, 2048], P('exp')
- g_value: float32 [2048, 2048], P('exp')
- g_output: float32 [2048, 2048], P('exp')
- g_router: float32 [2048, 16], P('exp')
- g_gains: float32 [2048, 4], P('exp')
- g_gate_up: float32 [16, 4096, 1024], P('exp', None, 'ctx')
- g_down: float32 [16, 2048, 1024], P('exp', None, 'ctx')
Inputs may be any that keep to these rules, and one draw needn't show every extreme that they name: `block_ids`: each row holds each block number once; the two blocks of one device add up to 7. `routes`: each token names 8 different experts.
All inputs are finite; a program needn't handle non-finite values.
Results may differ from a plain program's by a relative error of at most 0.025.
Values may be sent and summed in bfloat16 or wider, within the bound.
A program may use at most 448 MiB of HBM per device.

v0:
```python
import jax
import jax.numpy as jnp
from jax import lax
from jax.sharding import PartitionSpec as P

HEAD_DIM = 128
epsilon = 1e-05
rope_theta = 10000.0


def rms_scale(matrix, gain):
    return matrix * lax.rsqrt(jnp.mean(matrix * matrix, axis=-1, keepdims=True) + epsilon) * gain


def angle_tables(positions, head_width):
    half_width = head_width // 2
    inverse = rope_theta ** (-(jnp.arange(half_width, dtype=jnp.float32) * 2.0) / head_width)
    angles = positions.astype(jnp.float32)[:, None] * inverse[None, :]
    angles = jnp.concatenate([angles, angles], axis=-1)
    return (jnp.cos(angles), jnp.sin(angles))


def rotate(matrix, cosine, sine, head_count, head_width):
    row_count = matrix.shape[0]
    split_heads = matrix.reshape(row_count, head_count, head_width)
    half_width = head_width // 2
    turned = jnp.concatenate(
        [-split_heads[..., half_width:], split_heads[..., :half_width]], axis=-1
    )
    result = split_heads * cosine[:, None, :] + turned * sine[:, None, :]
    return result.reshape(row_count, head_count * head_width)


def all_positions(block_row, half_rows):
    offsets = jnp.arange(half_rows, dtype=jnp.int32)
    return (block_row[:, None] * half_rows + offsets[None, :]).reshape(-1)


def slot_table(route_rows, expert_count, capacity):
    flat_routes = route_rows.reshape(-1)
    onehot = (flat_routes[:, None] == jnp.arange(expert_count, dtype=jnp.int32)[None, :]).astype(
        jnp.int32
    )
    rank_of = jnp.sum(jnp.cumsum(onehot, axis=0) * onehot, axis=1) - 1
    kept_mask = rank_of < capacity
    pair_slot = jnp.where(kept_mask, flat_routes * capacity + rank_of, expert_count * capacity)
    return (pair_slot, kept_mask)


def per_device(
    layer_input,
    block_ids,
    routes,
    w_query,
    w_key,
    w_value,
    w_output,
    w_router,
    norm_gains,
    w_gate_up,
    w_down,
    d_out,
):
    query_full, key_full, value_full, output_full, router_full, gains_bf = (
        lax.all_gather(w_query, "exp", axis=0, tiled=True),
        lax.all_gather(w_key, "exp", axis=0, tiled=True),
        lax.all_gather(w_value, "exp", axis=0, tiled=True),
        lax.all_gather(w_output, "exp", axis=0, tiled=True),
        lax.all_gather(w_router, "exp", axis=0, tiled=True),
        lax.all_gather(norm_gains, "exp", axis=0, tiled=True),
    )
    gain_table = gains_bf.astype(jnp.float32)
    tokens = layer_input[0].astype(jnp.float32)
    row_count, model_width = tokens.shape
    head_width = HEAD_DIM
    head_count = model_width // head_width
    half_rows = row_count // 2
    key_positions = all_positions(block_ids[0], half_rows)
    device_index = lax.axis_index("ctx")
    query_positions = lax.dynamic_slice_in_dim(key_positions, device_index * row_count, row_count)
    cosine, sine = angle_tables(query_positions, head_width)
    score_scale = head_width ** (-0.5)

    def norm_rope(projected, gain):
        return rotate(rms_scale(projected, gain), cosine, sine, head_count, head_width)

    first_norm = rms_scale(tokens, gain_table[:, 0]).astype(jnp.bfloat16)
    query_pre = jnp.dot(first_norm, query_full, preferred_element_type=jnp.float32)
    key_pre = jnp.dot(first_norm, key_full, preferred_element_type=jnp.float32)
    own_values = jnp.dot(first_norm, value_full, preferred_element_type=jnp.float32).astype(
        jnp.bfloat16
    )
    query = norm_rope(query_pre, gain_table[:, 1]).astype(jnp.bfloat16)
    own_keys = norm_rope(key_pre, gain_table[:, 2]).astype(jnp.bfloat16)
    all_keys, all_values = (
        lax.all_gather(own_keys, "ctx", axis=0, tiled=True),
        lax.all_gather(own_values, "ctx", axis=0, tiled=True),
    )
    seq_length = all_keys.shape[0]
    query_heads = query.reshape(row_count, head_count, head_width)
    key_heads = all_keys.reshape(seq_length, head_count, head_width)
    value_heads = all_values.reshape(seq_length, head_count, head_width)
    visible = key_positions[None, :] <= query_positions[:, None]

    def scores_of():
        raw_scores = (
            jnp.einsum("qhd,khd->hqk", query_heads, key_heads, preferred_element_type=jnp.float32)
            * score_scale
        )
        return jnp.where(visible[None], raw_scores, -1e30)

    scores = scores_of()
    top_score = jnp.max(scores, axis=-1, keepdims=True)
    log_total = top_score + jnp.log(jnp.sum(jnp.exp(scores - top_score), axis=-1, keepdims=True))
    probs_low = jnp.exp(scores - log_total).astype(jnp.bfloat16)
    attended = (
        jnp.einsum("hqk,khd->qhd", probs_low, value_heads, preferred_element_type=jnp.float32)
        .reshape(row_count, model_width)
        .astype(jnp.bfloat16)
    )
    hidden = tokens + jnp.dot(attended, output_full, preferred_element_type=jnp.float32)
    second_norm = rms_scale(hidden, gain_table[:, 3]).astype(jnp.bfloat16)
    logits = jnp.dot(second_norm, router_full, preferred_element_type=jnp.float32)
    router_probs = jax.nn.softmax(logits, axis=-1)
    expert_count = router_full.shape[1]
    route_rows = routes[0]
    top_count = route_rows.shape[1]
    chosen_mask = (
        route_rows[..., None] == jnp.arange(expert_count, dtype=jnp.int32)[None, None, :]
    ).astype(jnp.float32)
    gates = jnp.sum(chosen_mask * router_probs[:, None, :], axis=-1)
    capacity = (5 * row_count * top_count + 4 * expert_count - 1) // (4 * expert_count)
    pair_slot, kept_mask = slot_table(route_rows, expert_count, capacity)
    slot_total = expert_count * capacity
    pair_rows = jnp.repeat(second_norm, top_count, axis=0)
    send_rows = jnp.zeros((slot_total + 1, model_width), jnp.bfloat16).at[pair_slot].set(pair_rows)
    send_rows = send_rows[:slot_total].reshape(expert_count, capacity, model_width)
    arrived = lax.all_to_all(send_rows, "exp", split_axis=0, concat_axis=1, tiled=True)
    gate_up_full, down_full = (
        lax.all_gather(w_gate_up, "ctx", axis=2, tiled=True),
        lax.all_gather(w_down, "ctx", axis=2, tiled=True),
    )
    gate_full = gate_up_full[:, :model_width]
    up_full = gate_up_full[:, model_width:]
    gate_pre = jnp.einsum("erd,edf->erf", arrived, gate_full, preferred_element_type=jnp.float32)
    up_pre = jnp.einsum("erd,edf->erf", arrived, up_full, preferred_element_type=jnp.float32)
    activated = jax.nn.silu(gate_pre)
    inner = (activated * up_pre).astype(jnp.bfloat16)
    expert_out = jnp.einsum(
        "erf,edf->erd", inner, down_full, preferred_element_type=jnp.float32
    ).astype(jnp.bfloat16)
    returned = lax.all_to_all(expert_out, "exp", split_axis=1, concat_axis=0, tiled=True)
    padded_out = jnp.concatenate(
        [returned.reshape(slot_total, model_width), jnp.zeros((1, model_width), jnp.bfloat16)],
        axis=0,
    )
    pair_out = padded_out[pair_slot].astype(jnp.float32).reshape(row_count, top_count, model_width)
    mixture = jnp.sum(gates[..., None] * pair_out, axis=1)
    output = (hidden + mixture).astype(jnp.bfloat16)[None]
    grad_out = d_out[0].astype(jnp.float32)
    pair_weight = jnp.where(kept_mask, gates.reshape(-1), 0.0)
    pair_grad = (pair_weight[:, None] * jnp.repeat(grad_out, top_count, axis=0)).astype(
        jnp.bfloat16
    )
    send_grad = jnp.zeros((slot_total + 1, model_width), jnp.bfloat16).at[pair_slot].set(pair_grad)
    send_grad = send_grad[:slot_total].reshape(expert_count, capacity, model_width)
    gate_grad = jnp.sum(pair_out * grad_out[:, None, :], axis=-1)
    out_grad = lax.all_to_all(send_grad, "exp", split_axis=0, concat_axis=1, tiled=True)
    gate_up_again, down_back = (
        lax.all_gather(w_gate_up, "ctx", axis=2, tiled=True),
        lax.all_gather(w_down, "ctx", axis=2, tiled=True),
    )
    gate_back = gate_up_again[:, :model_width]
    up_back = gate_up_again[:, model_width:]
    inner_grad = jnp.einsum("erd,edf->erf", out_grad, down_back, preferred_element_type=jnp.float32)
    sigmoid_gate = jax.nn.sigmoid(gate_pre)
    gate_pre_grad = (
        inner_grad * up_pre * sigmoid_gate * (1.0 + gate_pre * (1.0 - sigmoid_gate))
    ).astype(jnp.bfloat16)
    up_pre_grad = (inner_grad * activated).astype(jnp.bfloat16)
    down_grad = jnp.einsum("erd,erf->edf", out_grad, inner, preferred_element_type=jnp.float32)
    gate_w_grad = jnp.einsum(
        "erd,erf->edf", arrived, gate_pre_grad, preferred_element_type=jnp.float32
    )
    up_w_grad = jnp.einsum("erd,erf->edf", arrived, up_pre_grad, preferred_element_type=jnp.float32)
    arrived_grad = jnp.einsum(
        "erf,edf->erd", gate_pre_grad, gate_back, preferred_element_type=jnp.float32
    )
    arrived_grad = (
        arrived_grad
        + jnp.einsum("erf,edf->erd", up_pre_grad, up_back, preferred_element_type=jnp.float32)
    ).astype(jnp.bfloat16)
    gate_up_grad, down_grad_shard = (
        lax.psum_scatter(
            jnp.concatenate([gate_w_grad, up_w_grad], axis=1).astype(jnp.bfloat16),
            "ctx",
            scatter_dimension=2,
            tiled=True,
        ).astype(jnp.float32),
        lax.psum_scatter(
            down_grad.astype(jnp.bfloat16), "ctx", scatter_dimension=2, tiled=True
        ).astype(jnp.float32),
    )
    back_rows = lax.all_to_all(arrived_grad, "exp", split_axis=1, concat_axis=0, tiled=True)
    padded_back = jnp.concatenate(
        [back_rows.reshape(slot_total, model_width), jnp.zeros((1, model_width), jnp.bfloat16)],
        axis=0,
    )
    second_grad = jnp.sum(
        padded_back[pair_slot].astype(jnp.float32).reshape(row_count, top_count, model_width),
        axis=1,
    )
    prob_grad = jnp.sum(chosen_mask * gate_grad[..., None], axis=1)
    logit_grad = (
        router_probs * (prob_grad - jnp.sum(prob_grad * router_probs, axis=-1, keepdims=True))
    ).astype(jnp.bfloat16)
    second_grad = second_grad + jnp.einsum(
        "te,de->td", logit_grad, router_full, preferred_element_type=jnp.float32
    )
    second_value, second_back = jax.vjp(rms_scale, hidden, gain_table[:, 3])
    hidden_part, gain_two_grad = second_back(second_grad)
    hidden_grad = grad_out + hidden_part
    hidden_grad_low = hidden_grad.astype(jnp.bfloat16)
    attended_grad = jnp.einsum(
        "tf,df->td", hidden_grad_low, output_full, preferred_element_type=jnp.float32
    ).astype(jnp.bfloat16)
    attended_heads = attended_grad.reshape(row_count, head_count, head_width)
    probs_again = jnp.exp(scores_of() - log_total)
    probs_grad = jnp.einsum(
        "qhd,khd->hqk", attended_heads, value_heads, preferred_element_type=jnp.float32
    )
    row_dot = jnp.sum(probs_again * probs_grad, axis=-1, keepdims=True)
    score_grad = (probs_again * (probs_grad - row_dot)).astype(jnp.bfloat16)
    query_grad = (
        jnp.einsum(
            "hqk,khd->qhd", score_grad, key_heads, preferred_element_type=jnp.float32
        ).reshape(row_count, model_width)
        * score_scale
    )
    key_part = (
        jnp.einsum(
            "hqk,qhd->khd", score_grad, query_heads, preferred_element_type=jnp.float32
        ).reshape(seq_length, model_width)
        * score_scale
    )
    value_part = jnp.einsum(
        "hqk,qhd->khd",
        probs_again.astype(jnp.bfloat16),
        attended_heads,
        preferred_element_type=jnp.float32,
    ).reshape(seq_length, model_width)
    key_grad, value_grad = (
        lax.psum_scatter(
            key_part.astype(jnp.bfloat16), "ctx", scatter_dimension=0, tiled=True
        ).astype(jnp.float32),
        lax.psum_scatter(
            value_part.astype(jnp.bfloat16), "ctx", scatter_dimension=0, tiled=True
        ).astype(jnp.float32),
    )
    query_value, query_back = jax.vjp(norm_rope, query_pre, gain_table[:, 1])
    query_pre_grad, gain_query_grad = query_back(query_grad)
    key_value, key_back = jax.vjp(norm_rope, key_pre, gain_table[:, 2])
    key_pre_grad, gain_key_grad = key_back(key_grad)
    query_low = query_pre_grad.astype(jnp.bfloat16)
    key_low = key_pre_grad.astype(jnp.bfloat16)
    value_low = value_grad.astype(jnp.bfloat16)
    first_grad = jnp.einsum("tf,df->td", query_low, query_full, preferred_element_type=jnp.float32)
    first_grad = first_grad + jnp.einsum(
        "tf,df->td", key_low, key_full, preferred_element_type=jnp.float32
    )
    first_grad = first_grad + jnp.einsum(
        "tf,df->td", value_low, value_full, preferred_element_type=jnp.float32
    )
    first_value, first_back = jax.vjp(rms_scale, tokens, gain_table[:, 0])
    token_part, gain_one_grad = first_back(first_grad)
    input_grad = (hidden_grad + token_part)[None]
    gain_grads = jnp.stack([gain_one_grad, gain_query_grad, gain_key_grad, gain_two_grad], axis=1)
    query_w_grad = jnp.einsum(
        "td,tf->df", first_norm, query_low, preferred_element_type=jnp.float32
    )
    key_w_grad = jnp.einsum("td,tf->df", first_norm, key_low, preferred_element_type=jnp.float32)
    value_w_grad = jnp.einsum(
        "td,tf->df", first_norm, value_low, preferred_element_type=jnp.float32
    )
    output_w_grad = jnp.einsum(
        "td,tf->df", attended, hidden_grad_low, preferred_element_type=jnp.float32
    )
    router_grad = jnp.einsum(
        "td,te->de", second_norm, logit_grad, preferred_element_type=jnp.float32
    )
    query_share, key_share, value_share, output_share, router_share, gain_share = (
        lax.psum_scatter(
            query_w_grad.astype(jnp.bfloat16), "exp", scatter_dimension=0, tiled=True
        ).astype(jnp.float32),
        lax.psum_scatter(
            key_w_grad.astype(jnp.bfloat16), "exp", scatter_dimension=0, tiled=True
        ).astype(jnp.float32),
        lax.psum_scatter(
            value_w_grad.astype(jnp.bfloat16), "exp", scatter_dimension=0, tiled=True
        ).astype(jnp.float32),
        lax.psum_scatter(
            output_w_grad.astype(jnp.bfloat16), "exp", scatter_dimension=0, tiled=True
        ).astype(jnp.float32),
        lax.psum_scatter(
            router_grad.astype(jnp.bfloat16), "exp", scatter_dimension=0, tiled=True
        ).astype(jnp.float32),
        lax.psum_scatter(
            gain_grads.astype(jnp.bfloat16), "exp", scatter_dimension=0, tiled=True
        ).astype(jnp.float32),
    )
    query_sum, key_sum, value_sum, output_sum, router_sum, gain_sum = (
        lax.psum(query_share.astype(jnp.bfloat16), "ctx").astype(jnp.float32),
        lax.psum(key_share.astype(jnp.bfloat16), "ctx").astype(jnp.float32),
        lax.psum(value_share.astype(jnp.bfloat16), "ctx").astype(jnp.float32),
        lax.psum(output_share.astype(jnp.bfloat16), "ctx").astype(jnp.float32),
        lax.psum(router_share.astype(jnp.bfloat16), "ctx").astype(jnp.float32),
        lax.psum(gain_share.astype(jnp.bfloat16), "ctx").astype(jnp.float32),
    )
    return (
        output,
        input_grad,
        query_sum,
        key_sum,
        value_sum,
        output_sum,
        router_sum,
        gain_sum,
        gate_up_grad,
        down_grad_shard,
    )


def solution(mesh):
    in_specs = (
        P("exp", "ctx", None),
        P("exp", None),
        P("exp", "ctx", None),
        P("exp", None),
        P("exp", None),
        P("exp", None),
        P("exp", None),
        P("exp", None),
        P("exp", None),
        P("exp", None, "ctx"),
        P("exp", None, "ctx"),
        P("exp", "ctx", None),
    )
    out_specs = (
        P("exp", "ctx", None),
        P("exp", "ctx", None),
        P("exp", None),
        P("exp", None),
        P("exp", None),
        P("exp", None),
        P("exp", None),
        P("exp", None),
        P("exp", None, "ctx"),
        P("exp", None, "ctx"),
    )
    return jax.shard_map(
        per_device, mesh=mesh, in_specs=in_specs, out_specs=out_specs, check_vma=False
    )
```

profile of v0, /device:TPU:0, one launch (start us, length us, event | category | flops | bytes accessed | tf_op | source)
XLA Modules:
  0.0 3466.2 jit_solution(3763846171016239692)
XLA Ops:
  42.1 96.0 %all-gather.13.cloned.1.call-done = bf16[2048,2048]{1,0:T(8,128)(2,1)} async-done(((bf16[256,2048]{1,0:T(8,128)(2,1)}), bf16[2048,2048]{1,0:T(8,128)(2,1)}) %all-gather.13.cloned.1.call-update) | async-done | bytes 8388624 | tf_op jit(solution)/shard_map/all_gather | solution.py:65
  147.7 115.6 %all-gather.15.cloned.1.call-done = bf16[2048,2048]{1,0:T(8,128)(2,1)} async-done(((bf16[256,2048]{1,0:T(8,128)(2,1)}), bf16[2048,2048]{1,0:T(8,128)(2,1)}) %all-gather.15.cloned.1.call-update) | async-done | bytes 8388624 | tf_op jit(solution)/shard_map/all_gather | solution.py:66
  297.9 90.8 %all-gather.9.cloned.1.call-done = bf16[2048,2048]{1,0:T(8,128)(2,1)} async-done(((bf16[256,2048]{1,0:T(8,128)(2,1)}), bf16[2048,2048]{1,0:T(8,128)(2,1)}) %all-gather.9.cloned.1.call-update) | async-done | bytes 8388624 | tf_op jit(solution)/shard_map/all_gather | solution.py:67
  403.7 30.5 all_gather.39
  503.9 106.7 %all-gather.19.cloned.1.call-done = bf16[2048,2048]{1,0:T(8,128)(2,1)} async-done(((bf16[256,2048]{1,0:T(8,128)(2,1)}), bf16[2048,2048]{1,0:T(8,128)(2,1)}) %all-gather.19.cloned.1.call-update) | async-done | bytes 8388624 | tf_op jit(solution)/shard_map/all_gather | solution.py:68
  709.4 298.7 %all-to-all-done.2 = bf16[16,240,2048]{2,1,0:T(8,128)(2,1)} async-done(((bf16[16,240,2048]{2,1,0:T(8,128)(2,1)}), bf16[16,240,2048]{2,1,0:T(8,128)(2,1)}, u32[]{:S(2)}, u32[]{:S(2)}) %all-to-all-start.2) | async-done | bytes 15728672 | tf_op jit(solution)/shard_map/all_to_all | solution.py:168
  1028.7 324.3 %all-to-all-done = bf16[16,240,2048]{2,1,0:T(8,128)(2,1)} async-done(((bf16[16,240,2048]{2,1,0:T(8,128)(2,1)}), bf16[16,240,2048]{2,1,0:T(8,128)(2,1)}, u32[]{:S(2)}, u32[]{:S(2)}) %all-to-all-start) | async-done | bytes 15728672 | tf_op jit(solution)/shard_map/all_to_all | solution.py:138
  1411.3 32.9 multiply_convert_fusion.1
  1553.9 29.1 copy.133
  1583.1 258.1 %all-to-all-done.1 = bf16[2,1920,2048]{2,0,1:T(2,128)(2,1)} async-done(((bf16[2,1920,2048]{2,0,1:T(2,128)(2,1)}), bf16[2,1920,2048]{2,0,1:T(2,128)(2,1)}, u32[]{:S(2)}, u32[]{:S(2)}) %all-to-all-start.1) | async-done | bytes 15728672 | tf_op jit(solution)/shard_map/all_to_all | solution.py:152
  1865.9 31.5 gather_fusion
  1912.2 274.1 %all-to-all-done.3 = bf16[2,1920,2048]{2,0,1:T(2,128)(2,1)} async-done(((bf16[2,1920,2048]{2,0,1:T(2,128)(2,1)}), bf16[2,1920,2048]{2,0,1:T(2,128)(2,1)}, u32[]{:S(2)}, u32[]{:S(2)}) %all-to-all-start.3) | async-done | bytes 15728672 | tf_op jit(solution)/shard_map/all_to_all | solution.py:204
  2205.2 31.3 gather_fusion.1
  2287.5 31.7 multiply_reduce_fusion
  2319.2 32.1 multiply_convert_fusion
  2553.8 29.8 reduce-scatter.23.cloned.1.call-done
  2583.5 152.5 %reduce-scatter.17.cloned.1.call-done = bf16[256,2048]{1,0:T(8,128)(2,1)} async-done(((bf16[2048,2048]{1,0:T(8,128)(2,1)}), bf16[256,2048]{1,0:T(8,128)(2,1)}) %reduce-scatter.17.cloned.1.call-update) | async-done | bytes 1048592 | tf_op jit(solution)/shard_map/reduce_scatter | solution.py:292
  2736.0 151.7 %reduce-scatter.21.cloned.1.call-done = bf16[256,2048]{1,0:T(8,128)(2,1)} async-done(((bf16[2048,2048]{1,0:T(8,128)(2,1)}), bf16[256,2048]{1,0:T(8,128)(2,1)}) %reduce-scatter.21.cloned.1.call-update) | async-done | bytes 1048592 | tf_op jit(solution)/shard_map/reduce_scatter | solution.py:298
  2887.7 152.0 %reduce-scatter.19.cloned.1.call-done = bf16[256,2048]{1,0:T(8,128)(2,1)} async-done(((bf16[2048,2048]{1,0:T(8,128)(2,1)}), bf16[256,2048]{1,0:T(8,128)(2,1)}) %reduce-scatter.19.cloned.1.call-update) | async-done | bytes 1048592 | tf_op jit(solution)/shard_map/reduce_scatter | solution.py:295
  3039.7 73.1 %reduce-scatter.29.cloned.1.call-done = bf16[2,2048,256]{2,1,0:T(8,128)(2,1)} async-done(((bf16[2,2048,1024]{2,1,0:T(8,128)(2,1)}), bf16[2,2048,256]{2,1,0:T(8,128)(2,1)}) %reduce-scatter.29.cloned.1.call-update) | async-done | bytes 2097168 | tf_op jit(solution)/shard_map/reduce_scatter | solution.py:200
  3116.8 124.8 %reduce-scatter.27.cloned.1.call-done = bf16[2,4096,256]{2,1,0:T(8,128)(2,1)} async-done(((bf16[2,4096,1024]{2,1,0:T(8,128)(2,1)}), bf16[2,4096,256]{2,1,0:T(8,128)(2,1)}) %reduce-scatter.27.cloned.1.call-update) | async-done | bytes 4194320 | tf_op jit(solution)/shard_map/reduce_scatter | solution.py:194
  3250.6 56.8 %reduce-scatter.35.cloned.1.call-done = bf16[256,4]{1,0:T(8,128)(2,1)} async-done(((bf16[2048,4]{1,0:T(8,128)(2,1)}), bf16[256,4]{1,0:T(8,128)(2,1)}) %reduce-scatter.35.cloned.1.call-update) | async-done | bytes 2064
  3308.3 55.6 %reduce-scatter.25.cloned.1.call-done = bf16[256,16]{0,1:T(8,128)(2,1)} async-done(((bf16[2048,16]{0,1:T(8,128)(2,1)}), bf16[256,16]{0,1:T(8,128)(2,1)}) %reduce-scatter.25.cloned.1.call-update) | async-done | bytes 8208 | tf_op jit(solution)/shard_map/reduce_scatter | solution.py:304
  3375.3 76.6 %all-reduce.10.cloned.1.call-done = (bf16[256,2048]{1,0:T(8,128)(2,1)}, bf16[256,2048]{1,0:T(8,128)(2,1)}, bf16[256,2048]{1,0:T(8,128)(2,1)}, bf16[256,2048]{1,0:T(8,128)(2,1)}) async-done(((bf16[256,2048]{1,0:T(8,128)(2,1)}, bf16[256,2048]{1,0:T(8,128)(2,1)}, bf16[256,2048]{1,0:T(8,128)(2,1)}, bf16[256,2048]{1,0:T(8,128)(2,1)}), (bf16[256,2048]{1,0:T(8,128)(2,1)}, bf16[256,2048]{1,0:T(8,128)(2,1)}, ...) | async-done | bytes 4194320 | tf_op jit(solution)/shard_map/psum | solution.py:312
  (383 shorter events, 794.4 us)
Async XLA Ops:
  7.2 130.9 %all-gather.13.cloned.1.call-start = ((), (), s32[]{:S(2)}) async-start(), calls=%async_computation.16 | async-start | bytes 9437184 | tf_op jit(solution)/shard_map/all_gather | solution.py:65
  7.9 255.4 %all-gather.15.cloned.1.call-start = ((), (), s32[]{:S(2)}) async-start(), calls=%async_computation.17 | async-start | bytes 9437184 | tf_op jit(solution)/shard_map/all_gather | solution.py:66
  8.7 379.9 %all-gather.9.cloned.1.call-start = ((), (), s32[]{:S(2)}) async-start(), calls=%async_computation.14 | async-start | bytes 9437184 | tf_op jit(solution)/shard_map/all_gather | solution.py:67
  9.4 429.4 %all-gather.17.cloned.1.call-start = ((), (), s32[]{:S(2)}) async-start(), calls=%async_computation.18 | async-start | bytes 7864320 | tf_op jit(solution)/shard_map/all_gather | solution.py:96
  297.6 186.0 %all-gather.11.cloned.1.call-start = ((), (), s32[]{:S(2)}) async-start(), calls=%async_computation.15 | async-start | bytes 7864320 | tf_op jit(solution)/shard_map/all_gather | solution.py:97
  397.1 213.4 %all-gather.19.cloned.1.call-start = ((), (), s32[]{:S(2)}) async-start(), calls=%async_computation.19 | async-start | bytes 9437184 | tf_op jit(solution)/shard_map/all_gather | solution.py:68
  662.1 345.9 %all-to-all-start.2 = ((bf16[16,240,2048]{2,1,0:T(8,128)(2,1)}), bf16[16,240,2048]{2,1,0:T(8,128)(2,1)}, u32[]{:S(2)}, u32[]{:S(2)}) async-start(bf16[16,240,2048]{2,1,0:T(8,128)(2,1)} %bitcast.209), calls=%async_computation.2 | async-start | bytes 31457280 | tf_op jit(solution)/shard_map/all_to_all | solution.py:168
  667.8 698.7 %all-gather.21.cloned.1.call-start = ((), (), s32[]{:S(2)}) async-start(), calls=%async_computation.20 | async-start | bytes 20971520 | tf_op jit(solution)/shard_map/all_gather | solution.py:140
  1008.0 345.0 %all-to-all-start = ((bf16[16,240,2048]{2,1,0:T(8,128)(2,1)}), bf16[16,240,2048]{2,1,0:T(8,128)(2,1)}, u32[]{:S(2)}, u32[]{:S(2)}) async-start(bf16[16,240,2048]{2,1,0:T(8,128)(2,1)} %bitcast.208), calls=%async_computation | async-start | bytes 31457280 | tf_op jit(solution)/shard_map/all_to_all | solution.py:138
  1013.7 397.6 %all-gather.23.cloned.1.call-start = ((), (), s32[]{:S(2)}) async-start(), calls=%async_computation.21 | async-start | bytes 10485760 | tf_op jit(solution)/shard_map/all_gather | solution.py:141
  1496.8 344.4 %all-to-all-start.1 = ((bf16[2,1920,2048]{2,0,1:T(2,128)(2,1)}), bf16[2,1920,2048]{2,0,1:T(2,128)(2,1)}, u32[]{:S(2)}, u32[]{:S(2)}) async-start(bf16[2,1920,2048]{2,0,1:T(2,128)(2,1)} %copy.129), calls=%async_computation.1 | async-start | bytes 31457280 | tf_op jit(solution)/shard_map/all_to_all | solution.py:152
  1841.2 345.2 %all-to-all-start.3 = ((bf16[2,1920,2048]{2,0,1:T(2,128)(2,1)}), bf16[2,1920,2048]{2,0,1:T(2,128)(2,1)}, u32[]{:S(2)}, u32[]{:S(2)}) async-start(bf16[2,1920,2048]{2,0,1:T(2,128)(2,1)} %copy.133), calls=%async_computation.3 | async-start | bytes 31457280 | tf_op jit(solution)/shard_map/all_to_all | solution.py:204
  1846.9 570.9 %reduce-scatter.33.cloned.1.call-start = ((), (), s32[]{:S(2)}) async-start(), calls=%async_computation.30 | async-start | bytes 7864320
  1912.2 335.4 %copy-start.60 = (bf16[384,16]{0,1:T(8,128)(2,1)}, bf16[384,16]{0,1:T(8,128)(2,1)S(1)}, u32[]{:S(2)}) copy-start(bf16[384,16]{0,1:T(8,128)(2,1)S(1)} %multiply_convert_fusion.6) | copy-start | bytes 36868
  2287.4 143.5 %reduce-scatter.31.cloned.1.call-start = ((), (), s32[]{:S(2)}) async-start(), calls=%async_computation.29 | async-start | bytes 7864320
  2372.6 210.9 %reduce-scatter.23.cloned.1.call-start = ((), (), s32[]{:S(2)}) async-start(), calls=%async_computation.25 | async-start | bytes 9437184 | tf_op jit(solution)/shard_map/reduce_scatter | solution.py:301
  2383.2 352.9 %reduce-scatter.17.cloned.1.call-start = ((), (), s32[]{:S(2)}) async-start(), calls=%async_computation.22 | async-start | bytes 9437184 | tf_op jit(solution)/shard_map/reduce_scatter | solution.py:292
  2417.6 470.1 %reduce-scatter.21.cloned.1.call-start = ((), (), s32[]{:S(2)}) async-start(), calls=%async_computation.24 | async-start | bytes 9437184 | tf_op jit(solution)/shard_map/reduce_scatter | solution.py:298
  2427.4 612.3 %reduce-scatter.19.cloned.1.call-start = ((), (), s32[]{:S(2)}) async-start(), calls=%async_computation.23 | async-start | bytes 9437184 | tf_op jit(solution)/shard_map/reduce_scatter | solution.py:295
  2450.1 662.8 %reduce-scatter.29.cloned.1.call-start = ((), (), s32[]{:S(2)}) async-start(), calls=%async_computation.28 | async-start | bytes 10485760 | tf_op jit(solution)/shard_map/reduce_scatter | solution.py:200
  2474.2 767.4 %reduce-scatter.27.cloned.1.call-start = ((), (), s32[]{:S(2)}) async-start(), calls=%async_computation.27 | async-start | bytes 20971520 | tf_op jit(solution)/shard_map/reduce_scatter | solution.py:194
  2527.5 779.8 %reduce-scatter.35.cloned.1.call-start = ((), (), s32[]{:S(2)}) async-start(), calls=%async_computation.31 | async-start | bytes 589824
  2552.7 811.3 %reduce-scatter.25.cloned.1.call-start = ((), (), s32[]{:S(2)}) async-start(), calls=%async_computation.26 | async-start | bytes 73728 | tf_op jit(solution)/shard_map/reduce_scatter | solution.py:304
  2553.7 898.1 %all-reduce.10.cloned.1.call-start = ((), (), s32[]{:S(2)}) async-start(), calls=%async_computation.32 | async-start | bytes 8388608 | tf_op jit(solution)/shard_map/psum | solution.py:312
  (98 other events, 3224.1 us)
Sparse Core Ops, SparseCore 0:
  10.2 127.8 all-gather.12
  140.2 123.1 all-gather.14
  265.5 123.1 all-gather.8
  390.6 44.5 all-gather.16
  437.2 46.3 all-gather.10
  485.6 124.9 all-gather.18
  670.2 109.4 all-gather.20
  1016.1 60.6 all-gather.22
  2287.6 58.2 reduce-scatter.32
  2372.7 58.1 reduce-scatter.30
  2434.5 148.9 reduce-scatter.22
  2588.0 147.9 reduce-scatter.16
  2739.7 148.0 reduce-scatter.20
  2891.7 147.9 reduce-scatter.18
  3042.1 70.7 reduce-scatter.28
  3115.5 126.0 reduce-scatter.26
  3245.4 61.9 reduce-scatter.34
  3311.3 52.6 reduce-scatter.24
  3366.7 85.1 all-reduce.9
where the time goes:
time: 3480 us; the launch traced here: 3470 us
  waiting for transfers between devices  2450 us (70%)
  matrix products  426 us (12%)
  local copies, waits for them, and re-layouts  305 us (9%)
  other arithmetic  182 us (5%)
  blocking collectives  69 us (2%)
    all_to_all x1, waiting for transfers between devices, per_device(): lax.all_to_all(send_rows, 'exp', split_axis=0, concat_axis=1, tiled=True)  324 us
    all_to_all x1, waiting for transfers between devices, per_device(): lax.all_to_all(send_grad, 'exp', split_axis=0, concat_axis=1, tiled=True)  299 us
    all_to_all x1, waiting for transfers between devices, per_device(): lax.all_to_all(arrived_grad, 'exp', split_axis=1, concat_axis=0, tiled=True)  274 us
    all_to_all x1, waiting for transfers between devices, per_device(): lax.all_to_all(expert_out, 'exp', split_axis=1, concat_axis=0, tiled=True)  258 us
    reduce_scatter x1, waiting for transfers between devices, per_device(): lax.psum_scatter(query_w_grad.astype(jnp.bfloat16), 'exp', scatter_dimens...  153 us
    reduce_scatter x1, waiting for transfers between devices, per_device(): lax.psum_scatter(key_w_grad.astype(jnp.bfloat16), 'exp', scatter_dimensio...  152 us
    reduce_scatter x1, waiting for transfers between devices, per_device(): lax.psum_scatter(value_w_grad.astype(jnp.bfloat16), 'exp', scatter_dimens...  152 us
    reduce_scatter x1, waiting for transfers between devices, per_device(): lax.psum_scatter(jnp.concatenate([gate_w_grad, up_w_grad], axis=1).astype...  125 us
  transfers between devices with their start and end apart: 23, of which 19 were waited for; matrix products, arithmetic and copies ran while one was open for 19% of the time, Pallas kernels for 0%

commit v1 on v0

--- a/solution.py
+++ b/solution.py
@@ -2,6 +2,7 @@
 import jax.numpy as jnp
 from jax import lax
 from jax.sharding import PartitionSpec as P
+from jax.lax import axis_index, axis_size, ppermute
 
 HEAD_DIM = 128
 epsilon = 1e-05
@@ -61,10 +62,28 @@
     w_down,
     d_out,
 ):
+
+    def proceed_matrix(d0, inputs):
+        link_axis = "exp"
+        work_now = axis_size(link_axis)
+        e_now = axis_index(link_axis)
+        w_next, everything, b_now = (work_now, e_now, inputs.shape[d0])
+        sheets = [j * w_next if c == d0 else j for c, j in enumerate(inputs.shape)]
+        x_now = jnp.zeros(sheets, inputs.dtype)
+        block_next = lax.dynamic_update_slice_in_dim(x_now, inputs, everything * b_now, axis=d0)
+        for d in range(1, w_next):
+            inputs = ppermute(
+                inputs, link_axis, perm=[(c, (c + 1) % w_next) for c in range(w_next)]
+            )
+            block_next = lax.dynamic_update_slice_in_dim(
+                block_next, inputs, (everything - d) % w_next * b_now, axis=d0
+            )
+        return block_next
+
     query_full, key_full, value_full, output_full, router_full, gains_bf = (
         lax.all_gather(w_query, "exp", axis=0, tiled=True),
         lax.all_gather(w_key, "exp", axis=0, tiled=True),
-        lax.all_gather(w_value, "exp", axis=0, tiled=True),
+        proceed_matrix(0, w_value),
         lax.all_gather(w_output, "exp", axis=0, tiled=True),
         lax.all_gather(w_router, "exp", axis=0, tiled=True),
         lax.all_gather(norm_gains, "exp", axis=0, tiled=True),

time: 3480 us -> 3520 us (1.011)
    ppermute x0 -> x7, waiting for transfers between devices: none -> 167 us  [proceed_matrix(): ppermute(inputs, link_axis, perm=[(c, (c + 1) % w_next) for c in range(w_...]
    all_gather x1 -> x0, waiting for transfers between devices: 90.8 us -> none  [per_device(): lax.all_gather(w_value, 'exp', axis=0, tiled=True)]
    all_gather x1, waiting for transfers between devices: 107 us -> 64.5 us  [per_device(): lax.all_gather(w_output, 'exp', axis=0, tiled=True)]
  transfers between devices with their start and end apart: 23 -> 29, of which waited for: 19 -> 24; matrix products, arithmetic and copies ran while one was open for 19% -> 18% of each run, Pallas kernels for 0% -> 0%
where the time goes in v1:
time: 3520 us; the launch traced here: 3510 us
  waiting for transfers between devices  2480 us (70%)
  matrix products  425 us (12%)
  local copies, waits for them, and re-layouts  314 us (9%)
  other arithmetic  182 us (5%)
  blocking collectives  69 us (2%)
    all_to_all x1, waiting for transfers between devices, per_device(): lax.all_to_all(send_rows, 'exp', split_axis=0, concat_axis=1, tiled=True)  324 us
    all_to_all x1, waiting for transfers between devices, per_device(): lax.all_to_all(send_grad, 'exp', split_axis=0, concat_axis=1, tiled=True)  299 us
    all_to_all x1, waiting for transfers between devices, per_device(): lax.all_to_all(arrived_grad, 'exp', split_axis=1, concat_axis=0, tiled=True)  274 us
    all_to_all x1, waiting for transfers between devices, per_device(): lax.all_to_all(expert_out, 'exp', split_axis=1, concat_axis=0, tiled=True)  258 us
    ppermute x7, waiting for transfers between devices, proceed_matrix(): ppermute(inputs, link_axis, perm=[(c, (c + 1) % w_next) for c in range(w_...  167 us
    reduce_scatter x1, waiting for transfers between devices, per_device(): lax.psum_scatter(query_w_grad.astype(jnp.bfloat16), 'exp', scatter_dimens...  152 us
    reduce_scatter x1, waiting for transfers between devices, per_device(): lax.psum_scatter(key_w_grad.astype(jnp.bfloat16), 'exp', scatter_dimensio...  152 us
    reduce_scatter x1, waiting for transfers between devices, per_device(): lax.psum_scatter(value_w_grad.astype(jnp.bfloat16), 'exp', scatter_dimens...  152 us
  transfers between devices with their start and end apart: 29, of which 24 were waited for; matrix products, arithmetic and copies ran while one was open for 18% of the time, Pallas kernels for 0%

profile of v1, /device:TPU:0, one launch (start us, length us, event | category | flops | bytes accessed | tf_op | source)
XLA Modules:
  0.0 3505.2 jit_solution(7036273836250790285)
XLA Ops:
  12.1 28.3 all_gather.29
  42.0 96.0 %all-gather.10.cloned.1.call-done = bf16[2048,2048]{1,0:T(8,128)(2,1)} async-done(((bf16[256,2048]{1,0:T(8,128)(2,1)}), bf16[2048,2048]{1,0:T(8,128)(2,1)}) %all-gather.10.cloned.1.call-update) | async-done | bytes 8388624 | tf_op jit(solution)/shard_map/all_gather | solution.py:84
  147.7 115.6 %all-gather.12.cloned.1.call-done = bf16[2048,2048]{1,0:T(8,128)(2,1)} async-done(((bf16[256,2048]{1,0:T(8,128)(2,1)}), bf16[2048,2048]{1,0:T(8,128)(2,1)}) %all-gather.12.cloned.1.call-update) | async-done | bytes 8388624 | tf_op jit(solution)/shard_map/all_gather | solution.py:85
  485.4 30.5 all_gather.35
  585.1 64.5 %all-gather.16.cloned.1.call-done = bf16[2048,2048]{1,0:T(8,128)(2,1)} async-done(((bf16[256,2048]{1,0:T(8,128)(2,1)}), bf16[2048,2048]{1,0:T(8,128)(2,1)}) %all-gather.16.cloned.1.call-update) | async-done | bytes 8388624 | tf_op jit(solution)/shard_map/all_gather | solution.py:87
  748.4 298.7 %all-to-all-done.2 = bf16[16,240,2048]{2,1,0:T(8,128)(2,1)} async-done(((bf16[16,240,2048]{2,1,0:T(8,128)(2,1)}), bf16[16,240,2048]{2,1,0:T(8,128)(2,1)}, u32[]{:S(2)}, u32[]{:S(2)}) %all-to-all-start.2) | async-done | bytes 15728672 | tf_op jit(solution)/shard_map/all_to_all | solution.py:187
  1067.8 324.3 %all-to-all-done = bf16[16,240,2048]{2,1,0:T(8,128)(2,1)} async-done(((bf16[16,240,2048]{2,1,0:T(8,128)(2,1)}), bf16[16,240,2048]{2,1,0:T(8,128)(2,1)}, u32[]{:S(2)}, u32[]{:S(2)}) %all-to-all-start) | async-done | bytes 15728672 | tf_op jit(solution)/shard_map/all_to_all | solution.py:157
  1450.4 32.9 multiply_convert_fusion.1
  1506.7 29.1 copy.129
  1592.9 29.1 copy.133
  1622.1 258.2 %all-to-all-done.1 = bf16[2,1920,2048]{2,0,1:T(2,128)(2,1)} async-done(((bf16[2,1920,2048]{2,0,1:T(2,128)(2,1)}), bf16[2,1920,2048]{2,0,1:T(2,128)(2,1)}, u32[]{:S(2)}, u32[]{:S(2)}) %all-to-all-start.1) | async-done | bytes 15728672 | tf_op jit(solution)/shard_map/all_to_all | solution.py:171
  1905.0 31.5 gather_fusion
  1951.3 274.1 %all-to-all-done.3 = bf16[2,1920,2048]{2,0,1:T(2,128)(2,1)} async-done(((bf16[2,1920,2048]{2,0,1:T(2,128)(2,1)}), bf16[2,1920,2048]{2,0,1:T(2,128)(2,1)}, u32[]{:S(2)}, u32[]{:S(2)}) %all-to-all-start.3) | async-done | bytes 15728672 | tf_op jit(solution)/shard_map/all_to_all | solution.py:223
  2244.2 31.3 gather_fusion.1
  2326.7 31.9 multiply_reduce_fusion
  2358.6 32.1 multiply_convert_fusion
  2622.7 152.1 %reduce-scatter.17.cloned.1.call-done = bf16[256,2048]{1,0:T(8,128)(2,1)} async-done(((bf16[2048,2048]{1,0:T(8,128)(2,1)}), bf16[256,2048]{1,0:T(8,128)(2,1)}) %reduce-scatter.17.cloned.1.call-update) | async-done | bytes 1048592 | tf_op jit(solution)/shard_map/reduce_scatter | solution.py:311
  2774.9 151.5 %reduce-scatter.21.cloned.1.call-done = bf16[256,2048]{1,0:T(8,128)(2,1)} async-done(((bf16[2048,2048]{1,0:T(8,128)(2,1)}), bf16[256,2048]{1,0:T(8,128)(2,1)}) %reduce-scatter.21.cloned.1.call-update) | async-done | bytes 1048592 | tf_op jit(solution)/shard_map/reduce_scatter | solution.py:317
  2926.4 152.1 %reduce-scatter.19.cloned.1.call-done = bf16[256,2048]{1,0:T(8,128)(2,1)} async-done(((bf16[2048,2048]{1,0:T(8,128)(2,1)}), bf16[256,2048]{1,0:T(8,128)(2,1)}) %reduce-scatter.19.cloned.1.call-update) | async-done | bytes 1048592 | tf_op jit(solution)/shard_map/reduce_scatter | solution.py:314
  3078.5 73.2 %reduce-scatter.29.cloned.1.call-done = bf16[2,2048,256]{2,1,0:T(8,128)(2,1)} async-done(((bf16[2,2048,1024]{2,1,0:T(8,128)(2,1)}), bf16[2,2048,256]{2,1,0:T(8,128)(2,1)}) %reduce-scatter.29.cloned.1.call-update) | async-done | bytes 2097168 | tf_op jit(solution)/shard_map/reduce_scatter | solution.py:219
  3155.6 124.8 %reduce-scatter.27.cloned.1.call-done = bf16[2,4096,256]{2,1,0:T(8,128)(2,1)} async-done(((bf16[2,4096,1024]{2,1,0:T(8,128)(2,1)}), bf16[2,4096,256]{2,1,0:T(8,128)(2,1)}) %reduce-scatter.27.cloned.1.call-update) | async-done | bytes 4194320 | tf_op jit(solution)/shard_map/reduce_scatter | solution.py:213
  3289.4 56.8 %reduce-scatter.35.cloned.1.call-done = bf16[256,4]{1,0:T(8,128)(2,1)} async-done(((bf16[2048,4]{1,0:T(8,128)(2,1)}), bf16[256,4]{1,0:T(8,128)(2,1)}) %reduce-scatter.35.cloned.1.call-update) | async-done | bytes 2064
  3347.1 55.6 %reduce-scatter.25.cloned.1.call-done = bf16[256,16]{0,1:T(8,128)(2,1)} async-done(((bf16[2048,16]{0,1:T(8,128)(2,1)}), bf16[256,16]{0,1:T(8,128)(2,1)}) %reduce-scatter.25.cloned.1.call-update) | async-done | bytes 8208 | tf_op jit(solution)/shard_map/reduce_scatter | solution.py:323
  3414.1 76.4 %all-reduce.10.cloned.1.call-done = (bf16[256,2048]{1,0:T(8,128)(2,1)}, bf16[256,2048]{1,0:T(8,128)(2,1)}, bf16[256,2048]{1,0:T(8,128)(2,1)}, bf16[256,2048]{1,0:T(8,128)(2,1)}) async-done(((bf16[256,2048]{1,0:T(8,128)(2,1)}, bf16[256,2048]{1,0:T(8,128)(2,1)}, bf16[256,2048]{1,0:T(8,128)(2,1)}, bf16[256,2048]{1,0:T(8,128)(2,1)}), (bf16[256,2048]{1,0:T(8,128)(2,1)}, bf16[256,2048]{1,0:T(8,128)(2,1)}, ...) | async-done | bytes 4194320 | tf_op jit(solution)/shard_map/psum | solution.py:331
  (411 shorter events, 938.6 us)
Async XLA Ops:
  7.2 130.8 %all-gather.10.cloned.1.call-start = ((), (), s32[]{:S(2)}) async-start(), calls=%async_computation.15 | async-start | bytes 9437184 | tf_op jit(solution)/shard_map/all_gather | solution.py:84
  7.9 255.3 %all-gather.12.cloned.1.call-start = ((), (), s32[]{:S(2)}) async-start(), calls=%async_computation.16 | async-start | bytes 9437184 | tf_op jit(solution)/shard_map/all_gather | solution.py:85
  8.7 511.9 %all-gather.14.cloned.1.call-start = ((), (), s32[]{:S(2)}) async-start(), calls=%async_computation.17 | async-start | bytes 7864320 | tf_op jit(solution)/shard_map/all_gather | solution.py:115
  297.1 268.0 %all-gather.8.cloned.1.call-start = ((), (), s32[]{:S(2)}) async-start(), calls=%async_computation.14 | async-start | bytes 7864320 | tf_op jit(solution)/shard_map/all_gather | solution.py:116
  297.2 27.6 collective-permute-start
  324.8 26.3 collective-permute-start.1
  478.9 170.8 %all-gather.16.cloned.1.call-start = ((), (), s32[]{:S(2)}) async-start(), calls=%async_computation.18 | async-start | bytes 9437184 | tf_op jit(solution)/shard_map/all_gather | solution.py:87
  701.2 345.9 %all-to-all-start.2 = ((bf16[16,240,2048]{2,1,0:T(8,128)(2,1)}), bf16[16,240,2048]{2,1,0:T(8,128)(2,1)}, u32[]{:S(2)}, u32[]{:S(2)}) async-start(bf16[16,240,2048]{2,1,0:T(8,128)(2,1)} %bitcast.209), calls=%async_computation.2 | async-start | bytes 31457280 | tf_op jit(solution)/shard_map/all_to_all | solution.py:187
  706.9 698.7 %all-gather.18.cloned.1.call-start = ((), (), s32[]{:S(2)}) async-start(), calls=%async_computation.19 | async-start | bytes 20971520 | tf_op jit(solution)/shard_map/all_gather | solution.py:159
  1047.1 345.0 %all-to-all-start = ((bf16[16,240,2048]{2,1,0:T(8,128)(2,1)}), bf16[16,240,2048]{2,1,0:T(8,128)(2,1)}, u32[]{:S(2)}, u32[]{:S(2)}) async-start(bf16[16,240,2048]{2,1,0:T(8,128)(2,1)} %bitcast.208), calls=%async_computation | async-start | bytes 31457280 | tf_op jit(solution)/shard_map/all_to_all | solution.py:157
  1052.7 397.6 %all-gather.20.cloned.1.call-start = ((), (), s32[]{:S(2)}) async-start(), calls=%async_computation.20 | async-start | bytes 10485760 | tf_op jit(solution)/shard_map/all_gather | solution.py:160
  1535.9 344.4 %all-to-all-start.1 = ((bf16[2,1920,2048]{2,0,1:T(2,128)(2,1)}), bf16[2,1920,2048]{2,0,1:T(2,128)(2,1)}, u32[]{:S(2)}, u32[]{:S(2)}) async-start(bf16[2,1920,2048]{2,0,1:T(2,128)(2,1)} %copy.129), calls=%async_computation.1 | async-start | bytes 31457280 | tf_op jit(solution)/shard_map/all_to_all | solution.py:171
  1880.2 345.2 %all-to-all-start.3 = ((bf16[2,1920,2048]{2,0,1:T(2,128)(2,1)}), bf16[2,1920,2048]{2,0,1:T(2,128)(2,1)}, u32[]{:S(2)}, u32[]{:S(2)}) async-start(bf16[2,1920,2048]{2,0,1:T(2,128)(2,1)} %copy.133), calls=%async_computation.3 | async-start | bytes 31457280 | tf_op jit(solution)/shard_map/all_to_all | solution.py:223
  1885.9 571.2 %reduce-scatter.33.cloned.1.call-start = ((), (), s32[]{:S(2)}) async-start(), calls=%async_computation.29 | async-start | bytes 7864320
  2326.6 143.6 %reduce-scatter.31.cloned.1.call-start = ((), (), s32[]{:S(2)}) async-start(), calls=%async_computation.28 | async-start | bytes 7864320
  2412.0 210.7 %reduce-scatter.23.cloned.1.call-start = ((), (), s32[]{:S(2)}) async-start(), calls=%async_computation.24 | async-start | bytes 9437184 | tf_op jit(solution)/shard_map/reduce_scatter | solution.py:320
  2422.6 352.3 %reduce-scatter.17.cloned.1.call-start = ((), (), s32[]{:S(2)}) async-start(), calls=%async_computation.21 | async-start | bytes 9437184 | tf_op jit(solution)/shard_map/reduce_scatter | solution.py:311
  2457.0 469.3 %reduce-scatter.21.cloned.1.call-start = ((), (), s32[]{:S(2)}) async-start(), calls=%async_computation.23 | async-start | bytes 9437184 | tf_op jit(solution)/shard_map/reduce_scatter | solution.py:317
  2466.8 611.7 %reduce-scatter.19.cloned.1.call-start = ((), (), s32[]{:S(2)}) async-start(), calls=%async_computation.22 | async-start | bytes 9437184 | tf_op jit(solution)/shard_map/reduce_scatter | solution.py:314
  2489.3 662.3 %reduce-scatter.29.cloned.1.call-start = ((), (), s32[]{:S(2)}) async-start(), calls=%async_computation.27 | async-start | bytes 10485760 | tf_op jit(solution)/shard_map/reduce_scatter | solution.py:219
  2513.5 766.9 %reduce-scatter.27.cloned.1.call-start = ((), (), s32[]{:S(2)}) async-start(), calls=%async_computation.26 | async-start | bytes 20971520 | tf_op jit(solution)/shard_map/reduce_scatter | solution.py:213
  2566.8 779.4 %reduce-scatter.35.cloned.1.call-start = ((), (), s32[]{:S(2)}) async-start(), calls=%async_computation.30 | async-start | bytes 589824
  2594.4 808.3 %reduce-scatter.25.cloned.1.call-start = ((), (), s32[]{:S(2)}) async-start(), calls=%async_computation.25 | async-start | bytes 73728 | tf_op jit(solution)/shard_map/reduce_scatter | solution.py:323
  2595.5 895.0 %all-reduce.10.cloned.1.call-start = ((), (), s32[]{:S(2)}) async-start(), calls=%async_computation.31 | async-start | bytes 8388608 | tf_op jit(solution)/shard_map/psum | solution.py:331
  (108 other events, 3362.6 us)
Sparse Core Ops, SparseCore 0:
  10.2 127.7 all-gather.9
  140.1 123.1 all-gather.11
  297.2 44.5 all-gather.13
  479.0 43.6 all-gather.7
  524.7 124.9 all-gather.15
  709.0 109.4 all-gather.17
  1055.1 60.6 all-gather.19
  2326.7 58.2 reduce-scatter.32
  2412.1 58.0 reduce-scatter.30
  2473.7 149.0 reduce-scatter.22
  2626.8 147.9 reduce-scatter.16
  2778.3 147.9 reduce-scatter.20
  2930.4 147.9 reduce-scatter.18
  3080.9 70.7 reduce-scatter.28
  3154.3 126.0 reduce-scatter.26
  3284.2 61.9 reduce-scatter.34
  3350.0 52.6 reduce-scatter.24
  3405.3 85.1 all-reduce.9
